TPU v7x, 32 devices: a whole 2x2x4 slice. The times are simulated.
32 devices in a mesh: blk: 8 (over y, x, core), fsdp: 4 (over z).
Axes of the slice: x: 2, y: 2, z: 4, core: 2. Of those that a mesh axis runs over, the one named last changes fastest.
Arguments:
- hidden: bfloat16 [8, 512, 5120], P('blk', 'fsdp'), may hold values from -6 to 6
- grad_query: bfloat16 [8, 512, 5120], P('blk', 'fsdp'), may hold values from -6 to 6
- grad_value: bfloat16 [8, 512, 5120], P('blk', 'fsdp'), may hold values from -6 to 6
- adapters: bfloat16 [8, 192, 5120], P('blk', 'fsdp'), may hold values from -4 to 4
- first_moment: bfloat16 [8, 192, 5120], P('blk', 'fsdp'), may hold values from -0.009765625 to 0.009765625
- second_moment: bfloat16 [8, 192, 5120], P('blk', 'fsdp'), may hold values from 8.090865e-09 to 8.1025064e-08
- mixing: int32 [8, 3], P('blk'), may hold values from 1 to 2, as said below
Outputs:
- mixed: bfloat16 [8, 192, 5120], P('blk', 'fsdp')
Inputs may be any that keep to these rules, and one draw needn't show every extreme that they name: `mixing`: each row holds two numerators equal to 1 and one equal to 2.
All inputs are finite; a program needn't handle non-finite values.
Results may differ from a plain program's by a relative error of at most 0.0051.
Values may be sent and summed in bfloat16 or wider, within the bound.
A program may use at most 64 MiB of HBM per device.

v0:
```python
import math
import jax
import jax.numpy as jnp
from jax import lax
from jax.sharding import PartitionSpec as P

beta_one = 0.9
beta_two = 0.999
learn_rate = 0.2
decay_rate = 0.5
epsilon = 1e-08


def shifted(array, axis, by):
    length = lax.axis_size(axis)
    return lax.ppermute(array, axis, [(i, (i + by) % length) for i in range(length)])


def contract_tokens(left, right, scale):
    return (
        lax.dot_general(left, right, (((0,), (0,)), ((), ())), preferred_element_type=jnp.float32)
        * scale
    )


def shards(hidden, grad_query, grad_value, adapters, first_moment, second_moment, mixing):
    tokens = hidden[0]
    width = tokens.shape[1]
    full_rows = lax.all_gather(adapters, "fsdp", axis=1, tiled=True)[0]
    rank = full_rows.shape[0] // 4
    inv_width = 1.0 / math.sqrt(width)
    inv_rank = 1.0 / math.sqrt(rank)
    factors = []
    for index, cot in ((0, grad_query[0]), (1, grad_value[0])):
        down = full_rows[2 * index * rank : (2 * index + 1) * rank]
        up_rows = full_rows[(2 * index + 1) * rank : (2 * index + 2) * rank]
        lowrank = (jnp.dot(tokens, down.T, preferred_element_type=jnp.float32) * inv_width).astype(
            jnp.bfloat16
        )
        back = (jnp.dot(cot, up_rows.T, preferred_element_type=jnp.float32) * inv_rank).astype(
            jnp.bfloat16
        )
        factors.append((back, tokens, inv_width))
        factors.append((lowrank, cot, inv_rank))
    shard_rows = adapters.shape[1]
    group_tokens = tokens.shape[0] * lax.axis_size("fsdp")
    weights = mixing[0].astype(jnp.float32)
    term = jnp.concatenate(
        [contract_tokens(left, right, scale) for left, right, scale in factors], axis=0
    )

    def owned_rows(start, count, term=term):
        return term

    gradient = (
        lax.psum_scatter(
            owned_rows(jnp.int32(0), lax.axis_size("fsdp") * shard_rows).astype(jnp.bfloat16),
            "fsdp",
            scatter_dimension=0,
            tiled=True,
        ).astype(jnp.float32)
        / group_tokens
    )
    params = adapters[0].astype(jnp.float32)
    first = first_moment[0].astype(jnp.float32)
    second = second_moment[0].astype(jnp.float32)
    new_first = beta_one * first + (1.0 - beta_one) * gradient
    new_second = beta_two * second + (1.0 - beta_two) * gradient * gradient
    first_hat = new_first / (1.0 - beta_one**2)
    second_hat = new_second / (1.0 - beta_two**2)
    step = first_hat / (jnp.sqrt(second_hat) + epsilon) + decay_rate * params
    updated = (params - learn_rate * step).astype(jnp.bfloat16)
    lower = shifted(updated, "blk", 1)
    upper = shifted(updated, "blk", -1)
    total = weights[0] * lower.astype(jnp.float32) + weights[1] * updated.astype(jnp.float32)
    total = total + weights[2] * upper.astype(jnp.float32)
    results = (total / 4.0).astype(jnp.bfloat16)
    return results[None]


def solution(mesh):
    in_specs = (
        P("blk", "fsdp", None),
        P("blk", "fsdp", None),
        P("blk", "fsdp", None),
        P("blk", "fsdp", None),
        P("blk", "fsdp", None),
        P("blk", "fsdp", None),
        P("blk", None),
    )
    out_specs = P("blk", "fsdp", None)
    return jax.shard_map(shards, mesh=mesh, in_specs=in_specs, out_specs=out_specs, check_vma=False)
```

profile of v0, /device:TPU:1, one launch (start us, length us, event | category | flops | bytes accessed | tf_op | source)
XLA Modules:
  0.0 135.9 jit_solution(4167797149082029256)
XLA Ops:
  6.5 0.0 copy-start
  6.5 0.0 all-gather.2.cloned.1.call-start
  6.5 0.7 all-gather.2.cloned.1.call-update
  7.3 0.0 copy-start.1
  7.3 0.0 reduce-scatter.2.cloned.1.call-start
  7.3 47.3 %all-gather.2.cloned.1.call-done = bf16[1,192,5120]{2,1,0:T(8,128)(2,1)} async-done(((bf16[1,48,5120]{2,1,0:T(8,128)(2,1)}), bf16[1,192,5120]{2,1,0:T(8,128)(2,1)}) %all-gather.2.cloned.1.call-update) | async-done | bytes 1966096 | tf_op jit(solution)/shard_map/all_gather | solution.py:29
  54.6 0.0 copy-done
  54.6 2.5 %fusion = bf16[48,5120]{1,0:T(8,128)(2,1)S(1)} fusion(bf16[1,128,5120]{2,1,0:T(8,128)(2,1)S(1)} %copy-done, bf16[1,128,5120]{2,1,0:T(8,128)(2,1)} %param.8, bf16[1,192,5120]{2,1,0:T(8,128)(2,1)} %all-gather.2.cloned.1.call-done), kind=kOutput, calls=%fused_computation.4 | convolution fusion | flops 126332928 | bytes 3604480 | tf_op jit(solution)/shard_map/dot_general | solution.py:21
  57.2 0.0 copy-done.1
  57.2 2.9 %fusion.1 = bf16[48,5120]{1,0:T(8,128)(2,1)} fusion(bf16[1,128,5120]{2,1,0:T(8,128)(2,1)S(1)} %copy-done.1, bf16[1,128,5120]{2,1,0:T(8,128)(2,1)S(1)} %copy-done, bf16[1,192,5120]{2,1,0:T(8,128)(2,1)} %all-gather.2.cloned.1.call-done), kind=kOutput, calls=%fused_computation.5 | convolution fusion | flops 126332928 | bytes 3604480 | tf_op jit(solution)/shard_map/dot_general | solution.py:21
  60.1 0.0 copy-start.2
  60.1 3.4 %fusion.2 = bf16[48,5120]{1,0:T(8,128)(2,1)} fusion(bf16[1,128,5120]{2,1,0:T(8,128)(2,1)S(1)} %copy-done, bf16[1,128,5120]{2,1,0:T(8,128)(2,1)} %param.9, bf16[1,192,5120]{2,1,0:T(8,128)(2,1)} %all-gather.2.cloned.1.call-done), kind=kOutput, calls=%fused_computation.6 | convolution fusion | flops 126332928 | bytes 3604480 | tf_op jit(solution)/shard_map/dot_general | solution.py:21
  63.6 0.0 copy-done.2
  63.6 2.9 %fusion.3 = bf16[48,5120]{1,0:T(8,128)(2,1)} fusion(bf16[1,128,5120]{2,1,0:T(8,128)(2,1)S(1)} %copy-done.2, bf16[1,128,5120]{2,1,0:T(8,128)(2,1)S(1)} %copy-done, bf16[1,192,5120]{2,1,0:T(8,128)(2,1)} %all-gather.2.cloned.1.call-done), kind=kOutput, calls=%fused_computation.7 | convolution fusion | flops 126332928 | bytes 3604480 | tf_op jit(solution)/shard_map/dot_general | solution.py:21
  66.5 2.8 %pad_maximum_fusion = bf16[192,5120]{1,0:T(8,128)(2,1)} fusion(bf16[48,5120]{1,0:T(8,128)(2,1)} %fusion.3, bf16[48,5120]{1,0:T(8,128)(2,1)} %fusion.2, bf16[48,5120]{1,0:T(8,128)(2,1)} %fusion.1, bf16[48,5120]{1,0:T(8,128)(2,1)S(1)} %fusion), kind=kLoop, calls=%fused_computation.8 | loop fusion | flops 7864320 | bytes 3932160 | tf_op jit(solution)/shard_map/concatenate | solution.py:48
  69.2 0.0 copy-start.3
  69.2 0.0 copy-start.4
  69.2 0.0 copy-start.5
  69.2 0.0 reduce-scatter.2.cloned.1.call-update
  69.3 0.0 copy-start.6
  69.3 40.3 %reduce-scatter.2.cloned.1.call-done = bf16[48,5120]{1,0:T(8,128)(2,1)} async-done(((bf16[192,5120]{1,0:T(8,128)(2,1)}), bf16[48,5120]{1,0:T(8,128)(2,1)}) %reduce-scatter.2.cloned.1.call-update) | async-done | bytes 491536 | tf_op jit(solution)/shard_map/reduce_scatter | solution.py:56
  109.5 0.0 copy-done.3
  109.5 0.0 copy-done.4
  109.5 0.0 copy-done.5
  109.5 1.9 %fusion.50 = bf16[48,5120]{1,0:T(8,128)(2,1)S(1)} fusion(bf16[48,5120]{1,0:T(8,128)(2,1)} %reduce-scatter.2.cloned.1.call-done, bf16[1,48,5120]{2,1,0:T(8,128)(2,1)S(1)} %copy-done.4, bf16[1,48,5120]{2,1,0:T(8,128)(2,1)S(1)} %copy-done.5, bf16[1,48,5120]{2,1,0:T(8,128)(2,1)S(1)} %copy-done.3), kind=kLoop, calls=%fused_computation.36 | loop fusion | flops 5160960 | bytes 2457600 | tf_op jit(solution)/shard_map/convert_element_type | solution.py:72
  111.5 2.0 %collective-permute-start = (bf16[48,5120]{1,0:T(8,128)(2,1)S(1)}, bf16[48,5120]{1,0:T(8,128)(2,1)S(1)}, u32[]{:S(2)}, u32[]{:S(2)}) collective-permute-start(bf16[48,5120]{1,0:T(8,128)(2,1)S(1)} %fusion.50), channel_id=1, source_target_pairs={{0,4},{4,8},{8,12},{12,16},{16,20},{20,24},{24,28},{28,0},{1,5},{5... | collective-permute-start | bytes 1474568 | tf_op jit(solution)/shard_map/ppermute | solution.py:16
  113.5 0.0 collective-permute-start.1
  113.5 0.0 copy-done.6
  113.5 0.6 fusion.68
  114.1 8.6 %collective-permute-done = bf16[48,5120]{1,0:T(8,128)(2,1)S(1)} collective-permute-done((bf16[48,5120]{1,0:T(8,128)(2,1)S(1)}, bf16[48,5120]{1,0:T(8,128)(2,1)S(1)}, u32[]{:S(2)}, u32[]{:S(2)}) %collective-permute-start) | collective-permute-done | bytes 491552 | tf_op jit(solution)/shard_map/ppermute | solution.py:16
  122.7 3.5 %collective-permute-done.1 = bf16[48,5120]{1,0:T(8,128)(2,1)S(1)} collective-permute-done((bf16[48,5120]{1,0:T(8,128)(2,1)S(1)}, bf16[48,5120]{1,0:T(8,128)(2,1)S(1)}, u32[]{:S(2)}, u32[]{:S(2)}) %collective-permute-start.1) | collective-permute-done | bytes 491552 | tf_op jit(solution)/shard_map/ppermute | solution.py:16
  126.1 2.9 %fusion.59 = bf16[1,48,5120]{2,1,0:T(8,128)(2,1)} fusion(bf16[48,5120]{1,0:T(8,128)(2,1)S(1)} %collective-permute-done.1, bf16[48,5120]{1,0:T(8,128)(2,1)S(1)} %fusion.50, bf16[48,5120]{1,0:T(8,128)(2,1)S(1)} %collective-permute-done, f32[]{:T(128)} %bitcast.13, f32[]{:T(128)} %bitcast.12, f32[]{:T(128)} %bitcast), kind=kLoop, calls=%fused_computation.46 | loop fusion | flops 2457600 | bytes 1966092 | tf_op jit(solution)/shard_map/broadcast_in_dim | solution.py:78
  (1 shorter events, 0.0 us)
Async XLA Ops:
  6.5 48.1 %copy-start = (bf16[1,128,5120]{2,1,0:T(8,128)(2,1)S(1)}, bf16[1,128,5120]{2,1,0:T(8,128)(2,1)}, u32[]{:S(2)}) copy-start(bf16[1,128,5120]{2,1,0:T(8,128)(2,1)} %param.7) | copy-start | bytes 3932164
  6.5 48.1 %all-gather.2.cloned.1.call-start = ((), (), s32[]{:S(2)}) async-start(), calls=%async_computation.1 | async-start | bytes 2457600 | tf_op jit(solution)/shard_map/all_gather | solution.py:29
  7.3 49.9 %copy-start.1 = (bf16[1,128,5120]{2,1,0:T(8,128)(2,1)S(1)}, bf16[1,128,5120]{2,1,0:T(8,128)(2,1)}, u32[]{:S(2)}) copy-start(bf16[1,128,5120]{2,1,0:T(8,128)(2,1)} %param.8) | copy-start | bytes 3932164
  7.3 102.3 %reduce-scatter.2.cloned.1.call-start = ((), (), s32[]{:S(2)}) async-start(), calls=%async_computation.2 | async-start | bytes 2457600 | tf_op jit(solution)/shard_map/reduce_scatter | solution.py:56
  60.1 3.4 %copy-start.2 = (bf16[1,128,5120]{2,1,0:T(8,128)(2,1)S(1)}, bf16[1,128,5120]{2,1,0:T(8,128)(2,1)}, u32[]{:S(2)}) copy-start(bf16[1,128,5120]{2,1,0:T(8,128)(2,1)} %param.9) | copy-start | bytes 3932164
  69.2 40.3 %copy-start.3 = (bf16[1,48,5120]{2,1,0:T(8,128)(2,1)S(1)}, bf16[1,48,5120]{2,1,0:T(8,128)(2,1)}, u32[]{:S(2)}) copy-start(bf16[1,48,5120]{2,1,0:T(8,128)(2,1)} %param.10) | copy-start | bytes 1474564
  69.2 40.3 %copy-start.4 = (bf16[1,48,5120]{2,1,0:T(8,128)(2,1)S(1)}, bf16[1,48,5120]{2,1,0:T(8,128)(2,1)}, u32[]{:S(2)}) copy-start(bf16[1,48,5120]{2,1,0:T(8,128)(2,1)} %param.12) | copy-start | bytes 1474564
  69.2 40.3 %copy-start.5 = (bf16[1,48,5120]{2,1,0:T(8,128)(2,1)S(1)}, bf16[1,48,5120]{2,1,0:T(8,128)(2,1)}, u32[]{:S(2)}) copy-start(bf16[1,48,5120]{2,1,0:T(8,128)(2,1)} %param.11) | copy-start | bytes 1474564
  69.3 44.2 %copy-start.6 = (s32[1,3]{1,0:T(1,128)S(1)}, s32[1,3]{1,0:T(1,128)}, u32[]{:S(2)}) copy-start(s32[1,3]{1,0:T(1,128)} %param.13) | copy-start | bytes 40
  111.5 11.2 %collective-permute-start = (bf16[48,5120]{1,0:T(8,128)(2,1)S(1)}, bf16[48,5120]{1,0:T(8,128)(2,1)S(1)}, u32[]{:S(2)}, u32[]{:S(2)}) collective-permute-start(bf16[48,5120]{1,0:T(8,128)(2,1)S(1)} %fusion.50), channel_id=1, source_target_pairs={{0,4},{4,8},{8,12},{12,16},{16,20},{20,24},{24,28},{28,0},{1,5},{5... | collective-permute-start | bytes 1474568 | tf_op jit(solution)/shard_map/ppermute | solution.py:16
  113.5 12.7 %collective-permute-start.1 = (bf16[48,5120]{1,0:T(8,128)(2,1)S(1)}, bf16[48,5120]{1,0:T(8,128)(2,1)S(1)}, u32[]{:S(2)}, u32[]{:S(2)}) collective-permute-start(bf16[48,5120]{1,0:T(8,128)(2,1)S(1)} %fusion.50), channel_id=1, source_target_pairs={{0,28},{4,0},{8,4},{12,8},{16,12},{20,16},{24,20},{28,24},{1,29},{... | collective-permute-start | bytes 1474568 | tf_op jit(solution)/shard_map/ppermute | solution.py:16
Sparse Core Ops, SparseCore 0:
  8.9 45.6 all-gather.1
  69.4 40.0 reduce-scatter.1
where the time goes:
time: 136 us
  waiting for transfers between devices  100 us (74%)
  between operations  13.4 us (10%)
  matrix products  11.9 us (9%)
  other arithmetic  7.59 us (6%)
  starting transfers between devices  2.01 us (1%)
    all_gather x1, waiting for transfers between devices, shards(): full_rows = lax.all_gather(adapters, 'fsdp', axis=1, tiled=True)[0]  47.3 us
    reduce_scatter x1, waiting for transfers between devices, shards(): lax.psum_scatter(owned_rows(jnp.int32(0), lax.axis_size('fsdp') * shard_r...  40.3 us
    ppermute x2, waiting for transfers between devices, shifted(): lax.ppermute(array, axis, [(i, (i + by) % length) for i in range(length)])  12 us
    dot_general x4, matrix products, contract_tokens(): lax.dot_general(left, right, (((0,), (0,)), ((), ())), preferred_element_...  11.9 us
    broadcast_in_dim x1, other arithmetic, shards(): return results[None]  2.89 us
    concatenate x1, other arithmetic, shards(): jnp.concatenate([contract_tokens(left, right, scale) for left, right, sca...  2.75 us
  transfers between devices with their start and end apart: 4, of which 4 were waited for; matrix products, arithmetic and copies ran while one was open for 0% of the time, Pallas kernels for 0%

commit v1 on v0

--- a/solution.py
+++ b/solution.py
@@ -9,6 +9,19 @@
 learn_rate = 0.2
 decay_rate = 0.5
 epsilon = 1e-08
+
+
+def collect(value, axis, dim):
+    size, position, extent = (lax.axis_size(axis), lax.axis_index(axis), value.shape[dim])
+    ahead = [(i, (i + 1) % size) for i in range(size)]
+    filled = jnp.zeros((*value.shape[:dim], size * extent, *value.shape[dim + 1 :]), value.dtype)
+    held = value
+    for turn in range(size):
+        owner = (position - turn) % size
+        filled = lax.dynamic_update_slice_in_dim(filled, held, owner * extent, axis=dim)
+        if turn < size - 1:
+            held = lax.ppermute(held, axis, ahead)
+    return filled
 
 
 def shifted(array, axis, by):
@@ -26,7 +39,7 @@
 def shards(hidden, grad_query, grad_value, adapters, first_moment, second_moment, mixing):
     tokens = hidden[0]
     width = tokens.shape[1]
-    full_rows = lax.all_gather(adapters, "fsdp", axis=1, tiled=True)[0]
+    full_rows = collect(adapters, "fsdp", 1)[0]
     rank = full_rows.shape[0] // 4
     inv_width = 1.0 / math.sqrt(width)
     inv_rank = 1.0 / math.sqrt(rank)

time: 136 us -> 132 us (0.971)
  waiting for transfers between devices: 100 us -> 90.4 us
  local copies, waits for them, and re-layouts: 0.68 us -> 2.9 us
  starting transfers between devices: 2.01 us -> 4.1 us
    all_gather x1 -> x0, waiting for transfers between devices: 47.3 us -> none  [shards(): full_rows = lax.all_gather(adapters, 'fsdp', axis=1, tiled=True)[0]]
    ppermute x0 -> x3, waiting for transfers between devices: none -> 36.8 us  [collect(): held = lax.ppermute(held, axis, ahead)]
    ppermute x0 -> x3, starting transfers between devices: none -> 2.13 us  [collect(): held = lax.ppermute(held, axis, ahead)]
  transfers between devices with their start and end apart: 4 -> 6, of which waited for: 4 -> 6; matrix products, arithmetic and copies ran while one was open for 0% -> 2% of each run, Pallas kernels for 0% -> 0%
where the time goes in v1:
time: 132 us; the launch traced here: 131 us
  waiting for transfers between devices  90.4 us (68%)
  between operations  13.5 us (10%)
  matrix products  12.8 us (10%)
  other arithmetic  7.74 us (6%)
  starting transfers between devices  4.1 us (3%)
  local copies, waits for them, and re-layouts  2.9 us (2%)
    reduce_scatter x1, waiting for transfers between devices, shards(): lax.psum_scatter(owned_rows(jnp.int32(0), lax.axis_size('fsdp') * shard_r...  41.6 us
    ppermute x3, waiting for transfers between devices, collect(): held = lax.ppermute(held, axis, ahead)  36.8 us
    dot_general x4, matrix products, contract_tokens(): lax.dot_general(left, right, (((0,), (0,)), ((), ())), preferred_element_...  12.8 us
    ppermute x2, waiting for transfers between devices, shifted(): lax.ppermute(array, axis, [(i, (i + by) % length) for i in range(length)])  12 us
    broadcast_in_dim x1, other arithmetic, shards(): return results[None]  2.91 us
    concatenate x1, other arithmetic, shards(): jnp.concatenate([contract_tokens(left, right, scale) for left, right, sca...  2.89 us
  transfers between devices with their start and end apart: 6, of which 6 were waited for; matrix products, arithmetic and copies ran while one was open for 2% of the time, Pallas kernels for 0%

profile of v1, /device:TPU:1, one launch (start us, length us, event | category | flops | bytes accessed | tf_op | source)
XLA Modules:
  0.0 131.4 jit_solution(8146070024175631497)
XLA Ops:
  6.5 0.0 copy-start
  6.5 0.0 reduce-scatter.2.cloned.1.call-start
  6.5 2.1 %collective-permute-start = (bf16[1,48,5120]{2,1,0:T(8,128)(2,1)}, bf16[1,48,5120]{2,1,0:T(8,128)(2,1)}, u32[]{:S(2)}, u32[]{:S(2)}) collective-permute-start(bf16[1,48,5120]{2,1,0:T(8,128)(2,1)} %param.10), channel_id=1, source_target_pairs={{0,1},{1,2},{2,3},{3,0},{4,5},{5,6},{6,7},{7,4},{8,9},{9,10},{10,1... | collective-permute-start | bytes 1474568 | tf_op jit(solution)/shard_map/ppermute | solution.py:23
  8.7 0.0 copy-start.1
  8.7 0.2 squeeze.35
  8.9 0.9 copy-done.1
  9.8 12.1 %collective-permute-done = bf16[1,48,5120]{2,1,0:T(8,128)(2,1)} collective-permute-done((bf16[1,48,5120]{2,1,0:T(8,128)(2,1)}, bf16[1,48,5120]{2,1,0:T(8,128)(2,1)}, u32[]{:S(2)}, u32[]{:S(2)}) %collective-permute-start) | collective-permute-done | bytes 491552 | tf_op jit(solution)/shard_map/ppermute | solution.py:23
  22.0 0.0 collective-permute-start.1
  22.0 1.1 bitcast_dynamic-update-slice_fusion.2
  23.1 12.4 %collective-permute-done.1 = bf16[1,48,5120]{2,1,0:T(8,128)(2,1)S(1)} collective-permute-done((bf16[1,48,5120]{2,1,0:T(8,128)(2,1)}, bf16[1,48,5120]{2,1,0:T(8,128)(2,1)S(1)}, u32[]{:S(2)}, u32[]{:S(2)}) %collective-permute-start.1) | collective-permute-done | bytes 491552 | tf_op jit(solution)/shard_map/ppermute | solution.py:23
  35.4 0.0 collective-permute-start.2
  35.5 12.3 %collective-permute-done.2 = bf16[1,48,5120]{2,1,0:T(8,128)(2,1)S(1)} collective-permute-done((bf16[1,48,5120]{2,1,0:T(8,128)(2,1)S(1)}, bf16[1,48,5120]{2,1,0:T(8,128)(2,1)S(1)}, u32[]{:S(2)}, u32[]{:S(2)}) %collective-permute-start.2) | collective-permute-done | bytes 491552 | tf_op jit(solution)/shard_map/ppermute | solution.py:23
  47.9 0.0 copy-done
  47.9 3.2 %fusion = bf16[48,5120]{1,0:T(8,128)(2,1)} fusion(bf16[1,128,5120]{2,1,0:T(8,128)(2,1)S(1)} %copy-done, bf16[1,128,5120]{2,1,0:T(8,128)(2,1)} %param.8, bf16[192,5120]{1,0:T(8,128)(2,1)S(1)} %bitcast_dynamic-update-slice_fusion), kind=kOutput, calls=%fused_computation.4 | convolution fusion | flops 126332928 | bytes 3604480 | tf_op jit(solution)/shard_map/dot_general | solution.py:34
  51.0 3.2 %fusion.1 = bf16[48,5120]{1,0:T(8,128)(2,1)} fusion(bf16[1,128,5120]{2,1,0:T(8,128)(2,1)} %param.8, bf16[1,128,5120]{2,1,0:T(8,128)(2,1)S(1)} %copy-done, bf16[192,5120]{1,0:T(8,128)(2,1)S(1)} %bitcast_dynamic-update-slice_fusion), kind=kOutput, calls=%fused_computation.5 | convolution fusion | flops 126332928 | bytes 3604480 | tf_op jit(solution)/shard_map/dot_general | solution.py:34
  54.3 3.2 %fusion.2 = bf16[48,5120]{1,0:T(8,128)(2,1)} fusion(bf16[1,128,5120]{2,1,0:T(8,128)(2,1)S(1)} %copy-done, bf16[1,128,5120]{2,1,0:T(8,128)(2,1)} %param.9, bf16[192,5120]{1,0:T(8,128)(2,1)S(1)} %bitcast_dynamic-update-slice_fusion), kind=kOutput, calls=%fused_computation.6 | convolution fusion | flops 126332928 | bytes 3604480 | tf_op jit(solution)/shard_map/dot_general | solution.py:34
  57.4 3.2 %fusion.3 = bf16[48,5120]{1,0:T(8,128)(2,1)} fusion(bf16[1,128,5120]{2,1,0:T(8,128)(2,1)} %param.9, bf16[1,128,5120]{2,1,0:T(8,128)(2,1)S(1)} %copy-done, bf16[192,5120]{1,0:T(8,128)(2,1)S(1)} %bitcast_dynamic-update-slice_fusion), kind=kOutput, calls=%fused_computation.7 | convolution fusion | flops 126332928 | bytes 3604480 | tf_op jit(solution)/shard_map/dot_general | solution.py:34
  60.6 2.9 %pad_maximum_fusion = bf16[192,5120]{1,0:T(8,128)(2,1)} fusion(bf16[48,5120]{1,0:T(8,128)(2,1)} %fusion.3, bf16[48,5120]{1,0:T(8,128)(2,1)} %fusion.2, bf16[48,5120]{1,0:T(8,128)(2,1)} %fusion.1, bf16[48,5120]{1,0:T(8,128)(2,1)} %fusion), kind=kLoop, calls=%fused_computation.8 | loop fusion | flops 7864320 | bytes 3932160 | tf_op jit(solution)/shard_map/concatenate | solution.py:61
  63.5 0.0 copy-start.2
  63.5 0.0 copy-start.3
  63.5 0.0 copy-start.4
  63.5 0.0 copy-start.5
  63.5 0.0 reduce-scatter.2.cloned.1.call-update
  63.6 41.6 %reduce-scatter.2.cloned.1.call-done = bf16[48,5120]{1,0:T(8,128)(2,1)} async-done(((bf16[192,5120]{1,0:T(8,128)(2,1)}), bf16[48,5120]{1,0:T(8,128)(2,1)}) %reduce-scatter.2.cloned.1.call-update) | async-done | bytes 491536 | tf_op jit(solution)/shard_map/reduce_scatter | solution.py:69
  105.1 0.0 copy-done.2
  105.1 0.0 copy-done.3
  105.1 0.0 copy-done.4
  105.1 1.9 %fusion.50 = bf16[48,5120]{1,0:T(8,128)(2,1)S(1)} fusion(bf16[48,5120]{1,0:T(8,128)(2,1)} %reduce-scatter.2.cloned.1.call-done, bf16[1,48,5120]{2,1,0:T(8,128)(2,1)S(1)} %copy-done.3, bf16[1,48,5120]{2,1,0:T(8,128)(2,1)S(1)} %copy-done.4, bf16[1,48,5120]{2,1,0:T(8,128)(2,1)S(1)} %copy-done.2), kind=kLoop, calls=%fused_computation.36 | loop fusion | flops 5160960 | bytes 2457600 | tf_op jit(solution)/shard_map/convert_element_type | solution.py:85
  107.1 2.0 %collective-permute-start.3 = (bf16[48,5120]{1,0:T(8,128)(2,1)S(1)}, bf16[48,5120]{1,0:T(8,128)(2,1)S(1)}, u32[]{:S(2)}, u32[]{:S(2)}) collective-permute-start(bf16[48,5120]{1,0:T(8,128)(2,1)S(1)} %fusion.50), channel_id=1, source_target_pairs={{0,4},{4,8},{8,12},{12,16},{16,20},{20,24},{24,28},{28,0},{1,5},{5... | collective-permute-start | bytes 1474568 | tf_op jit(solution)/shard_map/ppermute | solution.py:29
  109.0 0.0 collective-permute-start.4
  109.0 0.0 copy-done.5
  109.0 0.6 fusion.76
  109.7 8.6 %collective-permute-done.3 = bf16[48,5120]{1,0:T(8,128)(2,1)S(1)} collective-permute-done((bf16[48,5120]{1,0:T(8,128)(2,1)S(1)}, bf16[48,5120]{1,0:T(8,128)(2,1)S(1)}, u32[]{:S(2)}, u32[]{:S(2)}) %collective-permute-start.3) | collective-permute-done | bytes 491552 | tf_op jit(solution)/shard_map/ppermute | solution.py:29
  118.2 3.4 %collective-permute-done.4 = bf16[48,5120]{1,0:T(8,128)(2,1)S(1)} collective-permute-done((bf16[48,5120]{1,0:T(8,128)(2,1)S(1)}, bf16[48,5120]{1,0:T(8,128)(2,1)S(1)}, u32[]{:S(2)}, u32[]{:S(2)}) %collective-permute-start.4) | collective-permute-done | bytes 491552 | tf_op jit(solution)/shard_map/ppermute | solution.py:29
  121.7 2.9 %fusion.59 = bf16[1,48,5120]{2,1,0:T(8,128)(2,1)} fusion(bf16[48,5120]{1,0:T(8,128)(2,1)S(1)} %collective-permute-done.4, bf16[48,5120]{1,0:T(8,128)(2,1)S(1)} %fusion.50, bf16[48,5120]{1,0:T(8,128)(2,1)S(1)} %collective-permute-done.3, f32[]{:T(128)} %bitcast.11, f32[]{:T(128)} %bitcast.10, f32[]{:T(128)} %bitcast), kind=kLoop, calls=%fused_computation.46 | loop fusion | flops 2457600 | bytes 1966092 | tf_op jit(solution)/shard_map/broadcast_in_dim | solution.py:91
  (4 shorter events, 0.1 us)
Async XLA Ops:
  6.5 41.3 %copy-start = (bf16[1,128,5120]{2,1,0:T(8,128)(2,1)S(1)}, bf16[1,128,5120]{2,1,0:T(8,128)(2,1)}, u32[]{:S(2)}) copy-start(bf16[1,128,5120]{2,1,0:T(8,128)(2,1)} %param.7) | copy-start | bytes 3932164
  6.5 98.6 %reduce-scatter.2.cloned.1.call-start = ((), (), s32[]{:S(2)}) async-start(), calls=%async_computation.1 | async-start | bytes 2457600 | tf_op jit(solution)/shard_map/reduce_scatter | solution.py:69
  6.5 15.4 %collective-permute-start = (bf16[1,48,5120]{2,1,0:T(8,128)(2,1)}, bf16[1,48,5120]{2,1,0:T(8,128)(2,1)}, u32[]{:S(2)}, u32[]{:S(2)}) collective-permute-start(bf16[1,48,5120]{2,1,0:T(8,128)(2,1)} %param.10), channel_id=1, source_target_pairs={{0,1},{1,2},{2,3},{3,0},{4,5},{5,6},{6,7},{7,4},{8,9},{9,10},{10,1... | collective-permute-start | bytes 1474568 | tf_op jit(solution)/shard_map/ppermute | solution.py:23
  8.7 1.1 copy-start.1
  22.0 13.5 %collective-permute-start.1 = (bf16[1,48,5120]{2,1,0:T(8,128)(2,1)}, bf16[1,48,5120]{2,1,0:T(8,128)(2,1)S(1)}, u32[]{:S(2)}, u32[]{:S(2)}) collective-permute-start(bf16[1,48,5120]{2,1,0:T(8,128)(2,1)} %collective-permute-done), channel_id=1, source_target_pairs={{0,1},{1,2},{2,3},{3,0},{4,5},{5,6},{6,7},{7,4},{8,9},{9,10},{10,1... | collective-permute-start | bytes 1474568 | tf_op jit(solution)/shard_map/ppermute | solution.py:23
  35.4 12.4 %collective-permute-start.2 = (bf16[1,48,5120]{2,1,0:T(8,128)(2,1)S(1)}, bf16[1,48,5120]{2,1,0:T(8,128)(2,1)S(1)}, u32[]{:S(2)}, u32[]{:S(2)}) collective-permute-start(bf16[1,48,5120]{2,1,0:T(8,128)(2,1)S(1)} %collective-permute-done.1), channel_id=1, source_target_pairs={{0,1},{1,2},{2,3},{3,0},{4,5},{5,6},{6,7},{7,4},{8,9},{9,10},{10,1... | collective-permute-start | bytes 1474568 | tf_op jit(solution)/shard_map/ppermute | solution.py:23
  63.5 41.6 %copy-start.2 = (bf16[1,48,5120]{2,1,0:T(8,128)(2,1)S(1)}, bf16[1,48,5120]{2,1,0:T(8,128)(2,1)}, u32[]{:S(2)}) copy-start(bf16[1,48,5120]{2,1,0:T(8,128)(2,1)} %param.10) | copy-start | bytes 1474564
  63.5 41.6 %copy-start.3 = (bf16[1,48,5120]{2,1,0:T(8,128)(2,1)S(1)}, bf16[1,48,5120]{2,1,0:T(8,128)(2,1)}, u32[]{:S(2)}) copy-start(bf16[1,48,5120]{2,1,0:T(8,128)(2,1)} %param.12) | copy-start | bytes 1474564
  63.5 41.6 %copy-start.4 = (bf16[1,48,5120]{2,1,0:T(8,128)(2,1)S(1)}, bf16[1,48,5120]{2,1,0:T(8,128)(2,1)}, u32[]{:S(2)}) copy-start(bf16[1,48,5120]{2,1,0:T(8,128)(2,1)} %param.11) | copy-start | bytes 1474564
  63.5 45.5 %copy-start.5 = (s32[1,3]{1,0:T(1,128)S(1)}, s32[1,3]{1,0:T(1,128)}, u32[]{:S(2)}) copy-start(s32[1,3]{1,0:T(1,128)} %param.13) | copy-start | bytes 40
  107.1 11.2 %collective-permute-start.3 = (bf16[48,5120]{1,0:T(8,128)(2,1)S(1)}, bf16[48,5120]{1,0:T(8,128)(2,1)S(1)}, u32[]{:S(2)}, u32[]{:S(2)}) collective-permute-start(bf16[48,5120]{1,0:T(8,128)(2,1)S(1)} %fusion.50), channel_id=1, source_target_pairs={{0,4},{4,8},{8,12},{12,16},{16,20},{20,24},{24,28},{28,0},{1,5},{5... | collective-permute-start | bytes 1474568 | tf_op jit(solution)/shard_map/ppermute | solution.py:29
  109.0 12.7 %collective-permute-start.4 = (bf16[48,5120]{1,0:T(8,128)(2,1)S(1)}, bf16[48,5120]{1,0:T(8,128)(2,1)S(1)}, u32[]{:S(2)}, u32[]{:S(2)}) collective-permute-start(bf16[48,5120]{1,0:T(8,128)(2,1)S(1)} %fusion.50), channel_id=1, source_target_pairs={{0,28},{4,0},{8,4},{12,8},{16,12},{20,16},{24,20},{28,24},{1,29},{... | collective-permute-start | bytes 1474568 | tf_op jit(solution)/shard_map/ppermute | solution.py:29
Sparse Core Ops, SparseCore 0:
  63.7 41.3 reduce-scatter.1
